TPU v7x, 32 devices: a whole 2x2x4 slice. The times are simulated.
32 devices in a mesh: panel: 2 (over y), gx: 16 (over z, x, core).
Axes of the slice: x: 2, y: 2, z: 4, core: 2. Of those that a mesh axis runs over, the one named last changes fastest.
Arguments:
- right_side: float32 [20, 1024, 256], P(None, 'gx', 'panel'), may hold values from -40 to 40
- previous: float32 [20, 1024, 256], P(None, 'gx', 'panel'), may hold values from -1.8 to 1.8
- diagonal: float32 [20, 1024, 256], P(None, 'gx', 'panel'), may hold values from 0.5 to 2
- vertical: float32 [19, 1024, 256], P(None, 'gx', 'panel'), may hold values from 0.5 to 2
- metric_a: float32 [1024, 256], P('gx', 'panel'), may hold values from 0.5 to 2
- metric_b: float32 [1024, 256], P('gx', 'panel'), may hold values from 0.5 to 2
- profile: float32 [20], replicated, may hold values from 0.5 to 2
- column_inverse: bfloat16 [4, 20, 1024, 256], P(None, None, 'gx', 'panel'), may hold values from -0.125 to 0.625, as said below
- edge_turn: int32 [4, 16, 2], replicated, may hold values from 0 to 3
Outputs:
- increment: float32 [20, 1024, 256], P(None, 'gx', 'panel')
Inputs may be any that keep to these rules, and one draw needn't show every extreme that they name: Entry column_inverse[c, k] lies in row k mod 4, column c of the inverse of the block of 4 levels that holds level k. `edge_turn`: entries 0 and 2 are read only for their lowest bit; entries 1 and 3 reverse with the lowest bit and negate with the value 2 bit.
All inputs are finite; a program needn't handle non-finite values.
Results may differ from a plain program's by a relative error of at most 0.0003.
Values sent between devices are 32-bit elements; how exact they have to be, the bound alone decides.
A program may use at most 64 MiB of HBM per device.

v0:
```python
import jax
import jax.numpy as jnp
from jax import lax
from jax.sharding import PartitionSpec as P

BK = 4


def from_behind(block, axis, distance):
    devices = range(lax.axis_size(axis))
    route = [((i - distance) % len(devices), i) for i in devices]
    return lax.ppermute(block, axis, route)


def flip_where(condition, values, dimension):
    return jnp.where(condition, jnp.flip(values, dimension), values)


def orient(values, code):
    turned = flip_where(code % 2 == 1, values, 1)
    return jnp.where(code // 2 == 1, -turned, turned)


def from_gx(values, offset):
    return from_behind(values, "gx", offset)


def from_panel(values, offset):
    return from_behind(values, "panel", offset)


def assemble(pressure, diagonal, vertical, flux_a, flux_b, high_a, high_b):
    next_a = jnp.concatenate([flux_a[:, 1:], high_a[:, None]], axis=1)
    next_b = jnp.concatenate([flux_b[:, :, 1:], high_b[:, :, None]], axis=2)
    vertical_flux = vertical * (pressure[1:] - pressure[:-1])
    zeros_row = jnp.zeros((1,) + pressure.shape[1:], jnp.float32)
    upward = jnp.concatenate([zeros_row, vertical_flux], axis=0) - jnp.concatenate(
        [vertical_flux, zeros_row], axis=0
    )
    return diagonal * pressure + (flux_a - next_a + flux_b - next_b) + upward


def local_fluxes(pressure, low_a, low_b, face_a, face_b):
    prev_a = jnp.concatenate([low_a[:, None], pressure[:, :-1]], axis=1)
    prev_b = jnp.concatenate([low_b[:, :, None], pressure[:, :, :-1]], axis=2)
    return (face_a * (pressure - prev_a), face_b * (pressure - prev_b))


def precondition(resid, column_inverse):
    level_count, rows_here, cols_here = resid.shape
    blocks = resid.reshape(level_count // BK, BK, rows_here, cols_here)
    inverse = column_inverse.reshape(BK, level_count // BK, BK, rows_here, cols_here)
    result = inverse[0].astype(jnp.float32) * blocks[:, 0:1]
    for column in range(1, BK):
        result = result + inverse[column].astype(jnp.float32) * blocks[:, column : column + 1]
    return result.reshape(level_count, rows_here, cols_here)


def shards(
    right_side, previous, diagonal, vertical, metric_a, metric_b, profile, column_inverse, edge_turn
):
    gx_index = lax.axis_index("gx")
    panel_index = lax.axis_index("panel")
    turns = edge_turn[:, gx_index, panel_index]
    face_a = metric_a[None] * profile[:, None, None]
    face_b = metric_b[None] * profile[:, None, None]

    def operate(pressure):
        low_a = flip_where(turns[0] % 2 == 1, from_gx(pressure[:, -1], 1), 1)
        low_b = flip_where(turns[2] % 2 == 1, from_panel(pressure[:, :, -1], 1), 1)
        flux_a, flux_b = local_fluxes(pressure, low_a, low_b, face_a, face_b)
        high_a = orient(from_gx(flux_a[:, 0], -1), turns[1])
        high_b = orient(from_panel(flux_b[:, :, 0], -1), turns[3])
        return assemble(pressure, diagonal, vertical, flux_a, flux_b, high_a, high_b)

    resid_first = right_side - operate(previous)
    search_first = precondition(resid_first, column_inverse)
    image_first = operate(search_first)
    cross_first, square_first = lax.psum(
        (jnp.sum(resid_first * image_first), jnp.sum(image_first * image_first)), ("panel", "gx")
    )
    alpha_first = cross_first / square_first
    resid_second = resid_first - alpha_first * image_first
    search_second = precondition(resid_second, column_inverse)
    image_second = operate(search_second)
    along_first, image_square, resid_image, resid_along = lax.psum(
        (
            jnp.sum(image_second * image_first),
            jnp.sum(image_second * image_second),
            jnp.sum(resid_second * image_second),
            jnp.sum(resid_second * image_first),
        ),
        ("panel", "gx"),
    )
    beta_coef = along_first / square_first
    alpha_second = (resid_image - beta_coef * resid_along) / (
        image_square - 2.0 * beta_coef * along_first + beta_coef * beta_coef * square_first
    )
    direction = search_second - beta_coef * search_first
    return alpha_first * search_first + alpha_second * direction


def solution(mesh):
    return jax.shard_map(
        shards,
        mesh=mesh,
        in_specs=(
            P(None, "gx", "panel"),
            P(None, "gx", "panel"),
            P(None, "gx", "panel"),
            P(None, "gx", "panel"),
            P("gx", "panel"),
            P("gx", "panel"),
            P(),
            P(None, None, "gx", "panel"),
            P(),
        ),
        out_specs=P(None, "gx", "panel"),
        check_vma=False,
    )
```

profile of v0, /device:TPU:14, one launch (start us, length us, event | category | flops | bytes accessed | tf_op | source)
XLA Modules:
  0.0 173.6 jit_solution(4378615325111884345)
XLA Ops:
  0.0 1.4 slice.165
  1.4 0.3 copy.413
  1.7 0.6 collective-permute-start.2
  2.2 0.4 copy.372
  2.7 1.3 copy_multiply_fusion.2
  4.1 1.0 fusion.26
  5.1 0.7 fusion.27
  14.1 0.9 slice.205
  15.2 1.3 copy.378
  16.5 2.0 %multiply_multiply_fusion.5 = (f32[20,64,128]{2,0,1:T(8,128)S(1)}, f32[20,64,128]{2,0,1:T(8,128)S(1)}) fusion(f32[20,63,128]{2,0,1:T(8,128)} %slice.205, f32[20,1,128]{2,0,1:T(8,128)S(1)} %select_bitcast_fusion.5, f32[20]{0:T(128)S(1)} %copy-done.15, f32[64,128]{1,0:T(8,128)S(1)} %copy-done.13, f32[20,64,128]{2,1,0:T(8,128)S(1)} %copy-done, ...), kind=kLoop, calls=%fused_computation.5 | loop fusion | flops 1310720 | bytes 3342416 | tf_op jit(solution)/shard_map/mul | solution.py:46
  18.5 0.3 copy.380
  18.8 1.6 collective-permute-start.3
  20.4 0.9 slice.206
  21.3 1.2 slice.209
  22.5 1.4 collective-permute-start.1
  24.0 1.3 copy.381
  25.4 3.8 %fusion.2 = f32[20,64,128]{2,0,1:T(8,128)S(1)} fusion(f32[20,64,128]{2,1,0:T(8,128)} %param.11, f32[20,64,128]{2,0,1:T(8,128)S(1)} %get-tuple-element.27, f32[20,64,128]{2,0,1:T(8,128)S(1)} %get-tuple-element.26, f32[20,1,128]{2,0,1:T(8,128)S(1)} %fusion.19, f32[20,63,128]{2,0,1:T(8,128)} %slice.206, f32[20,64,1]{2,0,1:T(8,128)} %copy.381, ...), kind=kLoop, calls=%fused_computation.22 | loop fusion | flops 1638400 | bytes 5865472 | tf_op jit(solution)/shard_map/sub | solution.py:76
  29.2 0.1 copy.387
  29.7 0.7 copy-done.6
  30.5 0.1 copy-done.8
  30.6 0.1 copy-done.10
  30.7 2.1 %fusion.9 = f32[20,64,128]{2,0,1:T(8,128)S(1)} fusion(f32[20,64,128]{2,1,0:T(8,128)S(1)} %bitcast.116, f32[20,64,128]{2,1,0:T(8,128)S(1)} %bitcast.118, f32[20,64,128]{2,1,0:T(8,128)S(1)} %bitcast.119, f32[20,64,128]{2,1,0:T(8,128)S(1)} %bitcast.115, bf16[1,20,64,128]{3,2,1,0:T(8,128)(2,1)S(1)} %copy-done.10, bf16[1,20,64,128]{3,2,1,0:T(8,128)(2,1)S(1)} %copy-done.8, ...), kind=kLoop, calls=%fused_computation.29 | loop fusion | flops 1802240 | bytes 4587520 | tf_op jit(solution)/shard_map/add | solution.py:55
  32.8 1.4 copy_multiply_fusion.1
  34.2 0.3 slice.221
  34.5 0.3 copy.396
  34.8 0.5 collective-permute-start.6
  35.3 0.9 slice.218
  36.3 2.3 %collective-permute-start.4 = (f32[20,128]{1,0:T(8,128)S(1)}, f32[20,128]{1,0:T(8,128)S(1)}, u32[]{:S(2)}, u32[]{:S(2)}) collective-permute-start(f32[20,128]{1,0:T(8,128)S(1)} %slice_bitcast_fusion.11), channel_id=1, source_target_pairs={{15,0},{0,1},{1,2},{2,3},{3,4},{4,5},{5,6},{6,7},{7,8},{8,9},{9,10... | collective-permute-start | bytes 30728 | tf_op jit(solution)/shard_map/ppermute | solution.py:12
  38.6 1.3 copy.397
  40.0 1.7 multiply_multiply_fusion.4
  41.7 0.9 copy.398
  42.6 1.5 collective-permute-start.7
  44.1 0.6 slice_bitcast_fusion.10
  44.7 1.0 slice.219
  45.7 1.2 slice.223
  46.8 0.8 rev.45
  47.6 0.7 fusion.22
  48.3 1.2 copy.399
  49.6 3.9 %multiply_reduce_fusion.4 = (f32[]{:T(128)}, f32[]{:T(128)}, f32[20,64,128]{2,0,1:T(8,128)S(1)}) fusion(f32[20,64,128]{2,0,1:T(8,128)S(1)} %fusion.2, f32[19,64,128]{2,0,1:T(8,128)} %copy_multiply_fusion.1, f32[20,64,1]{2,0,1:T(8,128)} %copy.399, f32[20,64,127]{2,0,1:T(8,128)} %slice.223, f32[20,64,128]{2,0,1:T(8,128)S(1)} %get-tuple-element.25, ...), kind=kLoop, calls=%fused_computation.57 | loop fusion | flops 2129918 | bytes 5865480 | tf_op jit(solution)/shard_map/reduce_sum | solution.py:80
  53.6 44.5 %all-reduce.7 = (f32[]{:T(128)}, f32[]{:T(128)}) all-reduce(f32[]{:T(128)} %get-tuple-element.10, f32[]{:T(128)} %get-tuple-element.9), channel_id=1, replica_groups=mesh['panel'=2,'gx'=16] {'panel','gx'}, use_global_device_ids=true, to_apply=%region_1.2 | all-reduce | flops 2 | bytes 16 | tf_op jit(solution)/shard_map/psum | solution.py:79
  99.5 0.1 copy.401
  99.7 0.7 copy-done.2
  100.7 0.7 copy-done.7
  101.5 0.1 copy-done.11
  101.6 2.1 %fusion.12 = f32[20,64,128]{2,0,1:T(8,128)S(1)} fusion(f32[20,64,128]{2,1,0:T(8,128)S(1)} %bitcast.113, f32[20,64,128]{2,1,0:T(8,128)S(1)} %bitcast.114, f32[20,64,128]{2,1,0:T(8,128)S(1)} %bitcast.117, f32[20,64,128]{2,1,0:T(8,128)S(1)} %bitcast.112, bf16[1,20,64,128]{3,2,1,0:T(8,128)(2,1)S(1)} %copy-done.11, bf16[1,20,64,128]{3,2,1,0:T(8,128)(2,1)S(1)} %copy-done.9, ...), kind=kLoop, calls=%fused_computation.32 | loop fusion | flops 1802240 | bytes 4587520 | tf_op jit(solution)/shard_map/add | solution.py:55
  103.8 1.4 copy_multiply_fusion
  105.2 0.3 slice.235
  105.5 0.3 copy.407
  105.8 1.1 collective-permute-start.10
  106.9 1.0 slice.232
  107.8 1.7 collective-permute-done.10
  109.6 1.2 copy.408
  110.8 0.1 collective-permute-done.8
  111.0 2.6 %multiply_multiply_fusion.3 = (f32[20,64,128]{2,0,1:T(8,128)}, f32[20,64,128]{2,0,1:T(8,128)S(1)}) fusion(f32[20,64,128]{2,0,1:T(8,128)S(1)} %fusion.12, f32[20,63,128]{2,0,1:T(8,128)} %slice.232, f32[20,1,128]{2,0,1:T(8,128)S(1)} %select_bitcast_fusion.1, f32[20]{0:T(128)S(1)} %copy-done.15, f32[64,128]{1,0:T(8,128)S(1)} %copy-done.13, ...), kind=kLoop, calls=%fused_computation.3 | loop fusion | flops 1310720 | bytes 3342416 | tf_op jit(solution)/shard_map/mul | solution.py:46
  113.6 0.3 copy.409
  113.9 1.0 collective-permute-start.11
  114.9 0.7 slice_bitcast_fusion.8
  115.6 2.1 %slice.233 = f32[20,63,128]{2,0,1:T(8,128)} slice(f32[20,64,128]{2,0,1:T(8,128)} %get-tuple-element.22), slice={[0:20], [1:64], [0:128]} | slice | bytes 1290240 | tf_op jit(solution)/shard_map/slice | solution.py:33
  117.7 1.2 slice.237
  119.0 1.2 copy.410
  120.4 4.3 %multiply_reduce_fusion = (f32[]{:T(128)}, f32[]{:T(128)}, f32[]{:T(128)}, f32[]{:T(128)}) fusion(f32[20,64,128]{2,0,1:T(8,128)S(1)} %get-tuple-element.17, f32[20,64,128]{2,0,1:T(8,128)} %copy-done.2, f32[19,64,128]{2,0,1:T(8,128)} %copy_multiply_fusion, f32[20,64,1]{2,0,1:T(8,128)} %copy.410, f32[20,64,127]{2,0,1:T(8,128)} %slice.237, ...), kind=kLoop, calls=%fused_computation.52 | loop fusion | flops 2785276 | bytes 5865488 | tf_op jit(solution)/shard_map/reduce_sum | solution.py:89
  124.6 43.4 %all-reduce.6 = (f32[]{:T(128)}, f32[]{:T(128)}, f32[]{:T(128)}, f32[]{:T(128)}) all-reduce(f32[]{:T(128)} %get-tuple-element.6, f32[]{:T(128)} %get-tuple-element.8, f32[]{:T(128)} %get-tuple-element.7, f32[]{:T(128)} %get-tuple-element.5), channel_id=1, replica_groups=mesh['panel'=2,'gx'=16] {'panel','gx'}, use_global_device_ids=true, to_apply=%region_7.8 | all-reduce | flops 4 | bytes 32 | tf_op jit(solution)/shard_map/psum | solution.py:86
  172.5 0.1 multiply_add_fusion
  172.6 1.0 copy.412
  (79 shorter events, 2.0 us)
Async XLA Ops:
  0.0 2.2 %copy-start = (f32[20,64,128]{2,1,0:T(8,128)S(1)}, f32[20,64,128]{2,1,0:T(8,128)}, u32[]{:S(2)}) copy-start(f32[20,64,128]{2,1,0:T(8,128)} %param.10) | copy-start | bytes 1966084
  1.4 1.3 copy-start.3
  1.7 13.4 %collective-permute-start.2 = (f32[20,64]{1,0:T(8,128)S(1)}, f32[20,64]{1,0:T(8,128)S(1)}, u32[]{:S(2)}, u32[]{:S(2)}) collective-permute-start(f32[20,64]{1,0:T(8,128)S(1)} %bitcast.126), channel_id=1, source_target_pairs={{16,0},{0,16},{17,1},{1,17},{18,2},{2,18},{19,3},{3,19},{20,4},{4,... | collective-permute-start | bytes 15368 | tf_op jit(solution)/shard_map/ppermute | solution.py:12
  2.6 13.8 %collective-permute-start = (f32[20,128]{1,0:T(8,128)S(1)}, f32[20,128]{1,0:T(8,128)S(1)}, u32[]{:S(2)}, u32[]{:S(2)}) collective-permute-start(f32[20,128]{1,0:T(8,128)S(1)} %slice_bitcast_fusion.13), channel_id=1, source_target_pairs={{15,0},{0,1},{1,2},{2,3},{3,4},{4,5},{5,6},{6,7},{7,8},{8,9},{9,10... | collective-permute-start | bytes 30728 | tf_op jit(solution)/shard_map/ppermute | solution.py:12
  2.7 1.3 copy-start.12
  4.1 1.0 copy-start.16
  5.7 10.8 %copy-start.13 = (f32[64,128]{1,0:T(8,128)S(1)}, f32[64,128]{1,0:T(8,128)}, u32[]{:S(2)}) copy-start(f32[64,128]{1,0:T(8,128)} %param.13) | copy-start | bytes 98308
  5.7 10.8 %copy-start.14 = (f32[64,128]{1,0:T(8,128)S(1)}, f32[64,128]{1,0:T(8,128)}, u32[]{:S(2)}) copy-start(f32[64,128]{1,0:T(8,128)} %param.14) | copy-start | bytes 98308
  5.7 10.8 %copy-start.15 = (f32[20]{0:T(128)S(1)}, f32[20]{0:T(128)}, u32[]{:S(2)}) copy-start(f32[20]{0:T(128)} %param.15) | copy-start | bytes 244
  18.8 5.1 %collective-permute-start.3 = (f32[20,64]{1,0:T(8,128)S(1)}, f32[20,64]{1,0:T(8,128)S(1)}, u32[]{:S(2)}, u32[]{:S(2)}) collective-permute-start(f32[20,64]{1,0:T(8,128)S(1)} %bitcast.122), channel_id=1, source_target_pairs={{16,0},{0,16},{17,1},{1,17},{18,2},{2,18},{19,3},{3,19},{20,4},{4,... | collective-permute-start | bytes 15368 | tf_op jit(solution)/shard_map/ppermute | solution.py:12
  22.5 2.8 %collective-permute-start.1 = (f32[20,128]{1,0:T(8,128)S(1)}, f32[20,128]{1,0:T(8,128)S(1)}, u32[]{:S(2)}, u32[]{:S(2)}) collective-permute-start(f32[20,128]{1,0:T(8,128)S(1)} %slice_bitcast_fusion.12), channel_id=1, source_target_pairs={{1,0},{2,1},{3,2},{4,3},{5,4},{6,5},{7,6},{8,7},{9,8},{10,9},{11,1... | collective-permute-start | bytes 30728 | tf_op jit(solution)/shard_map/ppermute | solution.py:12
  29.5 1.0 copy-start.6
  29.5 1.1 copy-start.8
  29.5 1.2 copy-start.10
  30.7 2.1 %copy-start.4 = (f32[19,64,128]{2,1,0:T(8,128)S(1)}, f32[19,64,128]{2,1,0:T(8,128)}, u32[]{:S(2)}) copy-start(f32[19,64,128]{2,1,0:T(8,128)} %param.12) | copy-start | bytes 1867780
  34.8 3.8 %collective-permute-start.6 = (f32[20,64]{1,0:T(8,128)S(1)}, f32[20,64]{1,0:T(8,128)S(1)}, u32[]{:S(2)}, u32[]{:S(2)}) collective-permute-start(f32[20,64]{1,0:T(8,128)S(1)} %bitcast.124), channel_id=1, source_target_pairs={{16,0},{0,16},{17,1},{1,17},{18,2},{2,18},{19,3},{3,19},{20,4},{4,... | collective-permute-start | bytes 15368 | tf_op jit(solution)/shard_map/ppermute | solution.py:12
  36.3 3.6 %collective-permute-start.4 = (f32[20,128]{1,0:T(8,128)S(1)}, f32[20,128]{1,0:T(8,128)S(1)}, u32[]{:S(2)}, u32[]{:S(2)}) collective-permute-start(f32[20,128]{1,0:T(8,128)S(1)} %slice_bitcast_fusion.11), channel_id=1, source_target_pairs={{15,0},{0,1},{1,2},{2,3},{3,4},{4,5},{5,6},{6,7},{7,8},{8,9},{9,10... | collective-permute-start | bytes 30728 | tf_op jit(solution)/shard_map/ppermute | solution.py:12
  41.7 5.2 %copy-start.1 = (f32[20,64,128]{2,0,1:T(8,128)}, f32[20,64,128]{2,0,1:T(8,128)S(1)}, u32[]{:S(2)}) copy-start(f32[20,64,128]{2,0,1:T(8,128)S(1)} %get-tuple-element.24) | copy-start | bytes 1966084
  42.6 4.2 %collective-permute-start.7 = (f32[20,64]{1,0:T(8,128)}, f32[20,64]{1,0:T(8,128)}, u32[]{:S(2)}, u32[]{:S(2)}) collective-permute-start(f32[20,64]{1,0:T(8,128)} %bitcast.31), channel_id=1, source_target_pairs={{16,0},{0,16},{17,1},{1,17},{18,2},{2,18},{19,3},{3,19},{20,4},{4,... | collective-permute-start | bytes 15368 | tf_op jit(solution)/shard_map/ppermute | solution.py:12
  46.8 2.7 %collective-permute-start.5 = (f32[20,128]{1,0:T(8,128)}, f32[20,128]{1,0:T(8,128)S(1)}, u32[]{:S(2)}, u32[]{:S(2)}) collective-permute-start(f32[20,128]{1,0:T(8,128)} %slice_bitcast_fusion.10), channel_id=1, source_target_pairs={{1,0},{2,1},{3,2},{4,3},{5,4},{6,5},{7,6},{8,7},{9,8},{10,9},{11,1... | collective-permute-start | bytes 30728 | tf_op jit(solution)/shard_map/ppermute | solution.py:12
  99.5 0.9 copy-start.2
  100.5 1.0 copy-start.7
  100.5 1.1 copy-start.9
  100.5 1.2 copy-start.11
  101.6 2.1 %copy-start.5 = (f32[19,64,128]{2,1,0:T(8,128)S(1)}, f32[19,64,128]{2,1,0:T(8,128)}, u32[]{:S(2)}) copy-start(f32[19,64,128]{2,1,0:T(8,128)} %param.12) | copy-start | bytes 1867780
  105.8 3.7 %collective-permute-start.10 = (f32[20,64]{1,0:T(8,128)S(1)}, f32[20,64]{1,0:T(8,128)S(1)}, u32[]{:S(2)}, u32[]{:S(2)}) collective-permute-start(f32[20,64]{1,0:T(8,128)S(1)} %bitcast.125), channel_id=1, source_target_pairs={{16,0},{0,16},{17,1},{1,17},{18,2},{2,18},{19,3},{3,19},{20,4},{4,... | collective-permute-start | bytes 15368 | tf_op jit(solution)/shard_map/ppermute | solution.py:12
  107.8 3.1 %collective-permute-start.8 = (f32[20,128]{1,0:T(8,128)S(1)}, f32[20,128]{1,0:T(8,128)S(1)}, u32[]{:S(2)}, u32[]{:S(2)}) collective-permute-start(f32[20,128]{1,0:T(8,128)S(1)} %slice_bitcast_fusion.9), channel_id=1, source_target_pairs={{15,0},{0,1},{1,2},{2,3},{3,4},{4,5},{5,6},{6,7},{7,8},{8,9},{9,10... | collective-permute-start | bytes 30728 | tf_op jit(solution)/shard_map/ppermute | solution.py:12
  113.9 4.9 %collective-permute-start.11 = (f32[20,64]{1,0:T(8,128)S(1)}, f32[20,64]{1,0:T(8,128)S(1)}, u32[]{:S(2)}, u32[]{:S(2)}) collective-permute-start(f32[20,64]{1,0:T(8,128)S(1)} %bitcast.123), channel_id=1, source_target_pairs={{16,0},{0,16},{17,1},{1,17},{18,2},{2,18},{19,3},{3,19},{20,4},{4,... | collective-permute-start | bytes 15368 | tf_op jit(solution)/shard_map/ppermute | solution.py:12
  118.9 1.4 collective-permute-start.9
where the time goes:
time: 175 us; the launch traced here: 174 us
  blocking collectives  87.9 us (50%)
  local copies, waits for them, and re-layouts  31.4 us (18%)
  other arithmetic  27.7 us (16%)
  between operations  14.6 us (8%)
  starting transfers between devices  10 us (6%)
  waiting for transfers between devices  1.99 us (1%)
    psum x1, blocking collectives, shards(): lax.psum((jnp.sum(resid_first * image_first), jnp.sum(image_first * image...  44.5 us
    psum x1, blocking collectives, shards(): lax.psum((jnp.sum(image_second * image_first), jnp.sum(image_second * ima...  43.4 us
    ppermute x12, starting transfers between devices, from_behind(): return lax.ppermute(block, axis, route)  10 us
    mul x3, other arithmetic, local_fluxes(): return (face_a * (pressure - prev_a), face_b * (pressure - prev_b))  6.31 us
    reduce_sum x1, other arithmetic, shards(): jnp.sum(image_second * image_second)  4.28 us
    add x2, other arithmetic, precondition(): result + inverse[column].astype(jnp.float32) * blocks[:, column:column + 1]  4.25 us
    mul x3, other arithmetic, assemble(): vertical_flux = vertical * (pressure[1:] - pressure[:-1])  4.12 us
    slice x3, local copies, waits for them, and re-layouts, assemble(): next_a = jnp.concatenate([flux_a[:, 1:], high_a[:, None]], axis=1)  3.94 us
  transfers between devices with their start and end apart: 12, of which 4 were waited for; matrix products, arithmetic and copies ran while one was open for 14% of the time, Pallas kernels for 0%

commit v1 on v0

--- a/solution.py
+++ b/solution.py
@@ -4,6 +4,11 @@
 from jax.sharding import PartitionSpec as P
 
 BK = 4
+
+
+def axis_by_axis(value, one, other):
+    partial = lax.psum(value, one)
+    return lax.psum(partial, other)
 
 
 def from_behind(block, axis, distance):
@@ -76,8 +81,8 @@
     resid_first = right_side - operate(previous)
     search_first = precondition(resid_first, column_inverse)
     image_first = operate(search_first)
-    cross_first, square_first = lax.psum(
-        (jnp.sum(resid_first * image_first), jnp.sum(image_first * image_first)), ("panel", "gx")
+    cross_first, square_first = axis_by_axis(
+        (jnp.sum(resid_first * image_first), jnp.sum(image_first * image_first)), "gx", "panel"
     )
     alpha_first = cross_first / square_first
     resid_second = resid_first - alpha_first * image_first

time: 175 us -> 175 us (level)
  blocking collectives: 87.9 us -> 85.1 us
  starting transfers between devices: 10 us -> 12.4 us
    psum x1 -> x2, blocking collectives: 44.5 us -> 31.8 us  [the longest x1 26 us: axis_by_axis(): partial = lax.psum(value, one)]
    psum x1, blocking collectives: 43.4 us -> 53.3 us  [shards(): lax.psum((jnp.sum(image_second * image_first), jnp.sum(image_second * ima...]
    ppermute x12, starting transfers between devices: 10 us -> 12.4 us  [from_behind(): return lax.ppermute(block, axis, route)]
where the time goes in v1:
time: 175 us; the launch traced here: 174 us
  blocking collectives  85.1 us (49%)
  local copies, waits for them, and re-layouts  31.4 us (18%)
  other arithmetic  27.7 us (16%)
  between operations  15.2 us (9%)
  starting transfers between devices  12.4 us (7%)
  waiting for transfers between devices  1.99 us (1%)
    psum x1, blocking collectives, shards(): lax.psum((jnp.sum(image_second * image_first), jnp.sum(image_second * ima...  53.3 us
    psum x1, blocking collectives, axis_by_axis(): partial = lax.psum(value, one)  26 us
    ppermute x12, starting transfers between devices, from_behind(): return lax.ppermute(block, axis, route)  12.4 us
    mul x3, other arithmetic, local_fluxes(): return (face_a * (pressure - prev_a), face_b * (pressure - prev_b))  6.29 us
    psum x1, blocking collectives, axis_by_axis(): return lax.psum(partial, other)  5.8 us
    reduce_sum x1, other arithmetic, shards(): jnp.sum(image_second * image_second)  4.25 us
    add x2, other arithmetic, precondition(): result + inverse[column].astype(jnp.float32) * blocks[:, column:column + 1]  4.25 us
    mul x3, other arithmetic, assemble(): vertical_flux = vertical * (pressure[1:] - pressure[:-1])  4.15 us
  transfers between devices with their start and end apart: 12, of which 4 were waited for; matrix products, arithmetic and copies ran while one was open for 14% of the time, Pallas kernels for 0%

profile of v1, /device:TPU:14, one launch (start us, length us, event | category | flops | bytes accessed | tf_op | source)
XLA Modules:
  0.0 173.7 jit_solution(14851721645743250254)
XLA Ops:
  0.0 1.4 slice.165
  1.4 0.3 copy.413
  1.7 0.6 collective-permute-start.2
  2.2 0.4 copy.372
  2.7 1.3 copy_multiply_fusion.2
  4.1 1.0 fusion.26
  5.1 0.7 fusion.27
  14.8 0.9 slice.205
  15.8 1.3 copy.378
  17.1 2.0 %multiply_multiply_fusion.5 = (f32[20,64,128]{2,0,1:T(8,128)S(1)}, f32[20,64,128]{2,0,1:T(8,128)S(1)}) fusion(f32[20,63,128]{2,0,1:T(8,128)} %slice.205, f32[20,1,128]{2,0,1:T(8,128)S(1)} %select_bitcast_fusion.5, f32[20]{0:T(128)S(1)} %copy-done.15, f32[64,128]{1,0:T(8,128)S(1)} %copy-done.13, f32[20,64,128]{2,1,0:T(8,128)S(1)} %copy-done, ...), kind=kLoop, calls=%fused_computation.5 | loop fusion | flops 1310720 | bytes 3342416 | tf_op jit(solution)/shard_map/mul | solution.py:51
  19.1 0.3 copy.380
  19.4 1.6 collective-permute-start.3
  21.0 0.9 slice.206
  21.9 1.1 slice.209
  23.1 1.4 collective-permute-start.1
  24.6 1.3 copy.381
  26.0 3.8 %fusion.2 = f32[20,64,128]{2,0,1:T(8,128)S(1)} fusion(f32[20,64,128]{2,1,0:T(8,128)} %param.11, f32[20,64,128]{2,0,1:T(8,128)S(1)} %get-tuple-element.29, f32[20,64,128]{2,0,1:T(8,128)S(1)} %get-tuple-element.28, f32[20,1,128]{2,0,1:T(8,128)S(1)} %fusion.19, f32[20,63,128]{2,0,1:T(8,128)} %slice.206, f32[20,64,1]{2,0,1:T(8,128)} %copy.381, ...), kind=kLoop, calls=%fused_computation.22 | loop fusion | flops 1638400 | bytes 5865472 | tf_op jit(solution)/shard_map/sub | solution.py:81
  29.8 0.1 copy.387
  30.3 0.7 copy-done.6
  31.2 0.1 copy-done.10
  31.3 2.1 %fusion.9 = f32[20,64,128]{2,0,1:T(8,128)S(1)} fusion(f32[20,64,128]{2,1,0:T(8,128)S(1)} %bitcast.116, f32[20,64,128]{2,1,0:T(8,128)S(1)} %bitcast.118, f32[20,64,128]{2,1,0:T(8,128)S(1)} %bitcast.119, f32[20,64,128]{2,1,0:T(8,128)S(1)} %bitcast.115, bf16[1,20,64,128]{3,2,1,0:T(8,128)(2,1)S(1)} %copy-done.10, bf16[1,20,64,128]{3,2,1,0:T(8,128)(2,1)S(1)} %copy-done.8, ...), kind=kLoop, calls=%fused_computation.29 | loop fusion | flops 1802240 | bytes 4587520 | tf_op jit(solution)/shard_map/add | solution.py:60
  33.4 1.4 copy_multiply_fusion.1
  34.8 0.3 slice.221
  35.1 0.3 copy.396
  35.4 0.5 collective-permute-start.6
  35.9 0.9 slice.218
  36.9 2.3 %collective-permute-start.4 = (f32[20,128]{1,0:T(8,128)S(1)}, f32[20,128]{1,0:T(8,128)S(1)}, u32[]{:S(2)}, u32[]{:S(2)}) collective-permute-start(f32[20,128]{1,0:T(8,128)S(1)} %slice_bitcast_fusion.11), channel_id=1, source_target_pairs={{15,0},{0,1},{1,2},{2,3},{3,4},{4,5},{5,6},{6,7},{7,8},{8,9},{9,10... | collective-permute-start | bytes 30728 | tf_op jit(solution)/shard_map/ppermute | solution.py:17
  39.2 1.3 copy.397
  40.5 1.7 multiply_multiply_fusion.4
  42.3 0.9 copy.398
  43.2 1.5 collective-permute-start.7
  44.7 0.6 slice_bitcast_fusion.10
  45.3 0.9 slice.219
  46.2 1.1 slice.223
  47.4 0.8 rev.45
  48.2 0.7 fusion.22
  48.9 1.2 copy.399
  50.2 3.9 %multiply_reduce_fusion.4 = (f32[]{:T(128)}, f32[]{:T(128)}, f32[20,64,128]{2,0,1:T(8,128)S(1)}) fusion(f32[20,64,128]{2,0,1:T(8,128)S(1)} %fusion.2, f32[19,64,128]{2,0,1:T(8,128)} %copy_multiply_fusion.1, f32[20,64,1]{2,0,1:T(8,128)} %copy.399, f32[20,64,127]{2,0,1:T(8,128)} %slice.223, f32[20,64,128]{2,0,1:T(8,128)S(1)} %get-tuple-element.27, ...), kind=kLoop, calls=%fused_computation.57 | loop fusion | flops 2129918 | bytes 5865480 | tf_op jit(solution)/shard_map/reduce_sum | solution.py:85
  54.1 26.0 %all-reduce.7 = (f32[]{:T(128)}, f32[]{:T(128)}) all-reduce(f32[]{:T(128)} %get-tuple-element.10, f32[]{:T(128)} %get-tuple-element.9), channel_id=1, replica_groups=mesh['panel'=2,'gx'=16] {'gx'}, use_global_device_ids=true, to_apply=%region_1.2 | all-reduce | flops 2 | bytes 16 | tf_op jit(solution)/shard_map/psum | solution.py:10
  80.1 5.8 %all-reduce.8 = (f32[]{:T(128)}, f32[]{:T(128)}) all-reduce(f32[]{:T(128)} %get-tuple-element.15, f32[]{:T(128)} %get-tuple-element.16), channel_id=1, replica_groups=mesh['panel'=2,'gx'=16] {'panel'}, use_global_device_ids=true, to_apply=%region_2.3 | all-reduce | flops 2 | bytes 16 | tf_op jit(solution)/shard_map/psum | solution.py:11
  87.3 0.1 copy.401
  87.5 0.7 copy-done.2
  88.5 0.7 copy-done.7
  89.4 2.1 %fusion.12 = f32[20,64,128]{2,0,1:T(8,128)S(1)} fusion(f32[20,64,128]{2,1,0:T(8,128)S(1)} %bitcast.113, f32[20,64,128]{2,1,0:T(8,128)S(1)} %bitcast.114, f32[20,64,128]{2,1,0:T(8,128)S(1)} %bitcast.117, f32[20,64,128]{2,1,0:T(8,128)S(1)} %bitcast.112, bf16[1,20,64,128]{3,2,1,0:T(8,128)(2,1)S(1)} %copy-done.11, bf16[1,20,64,128]{3,2,1,0:T(8,128)(2,1)S(1)} %copy-done.9, ...), kind=kLoop, calls=%fused_computation.32 | loop fusion | flops 1802240 | bytes 4587520 | tf_op jit(solution)/shard_map/add | solution.py:60
  91.6 1.4 copy_multiply_fusion
  93.0 0.3 slice.235
  93.3 0.3 copy.407
  93.6 1.3 collective-permute-start.10
  94.9 0.9 slice.232
  95.8 1.5 collective-permute-done.10
  97.4 1.2 copy.408
  98.6 0.3 collective-permute-done.8
  99.0 2.6 %multiply_multiply_fusion.3 = (f32[20,64,128]{2,0,1:T(8,128)}, f32[20,64,128]{2,0,1:T(8,128)S(1)}) fusion(f32[20,64,128]{2,0,1:T(8,128)S(1)} %fusion.12, f32[20,63,128]{2,0,1:T(8,128)} %slice.232, f32[20,1,128]{2,0,1:T(8,128)S(1)} %select_bitcast_fusion.1, f32[20]{0:T(128)S(1)} %copy-done.15, f32[64,128]{1,0:T(8,128)S(1)} %copy-done.13, ...), kind=kLoop, calls=%fused_computation.3 | loop fusion | flops 1310720 | bytes 3342416 | tf_op jit(solution)/shard_map/mul | solution.py:51
  101.6 0.3 copy.409
  101.9 1.0 collective-permute-start.11
  102.9 0.7 slice_bitcast_fusion.8
  103.6 2.1 %slice.233 = f32[20,63,128]{2,0,1:T(8,128)} slice(f32[20,64,128]{2,0,1:T(8,128)} %get-tuple-element.24), slice={[0:20], [1:64], [0:128]} | slice | bytes 1290240 | tf_op jit(solution)/shard_map/slice | solution.py:38
  105.7 1.2 slice.237
  106.8 2.2 %collective-permute-start.9 = (f32[20,128]{1,0:T(8,128)S(1)}, f32[20,128]{1,0:T(8,128)S(1)}, u32[]{:S(2)}, u32[]{:S(2)}) collective-permute-start(f32[20,128]{1,0:T(8,128)S(1)} %slice_bitcast_fusion.8), channel_id=1, source_target_pairs={{1,0},{2,1},{3,2},{4,3},{5,4},{6,5},{7,6},{8,7},{9,8},{10,9},{11,1... | collective-permute-start | bytes 30728 | tf_op jit(solution)/shard_map/ppermute | solution.py:17
  109.1 1.2 copy.410
  110.5 4.3 %multiply_reduce_fusion = (f32[]{:T(128)}, f32[]{:T(128)}, f32[]{:T(128)}, f32[]{:T(128)}) fusion(f32[20,64,128]{2,0,1:T(8,128)S(1)} %get-tuple-element.19, f32[20,64,128]{2,0,1:T(8,128)} %copy-done.2, f32[19,64,128]{2,0,1:T(8,128)} %copy_multiply_fusion, f32[20,64,1]{2,0,1:T(8,128)} %copy.410, f32[20,64,127]{2,0,1:T(8,128)} %slice.237, ...), kind=kLoop, calls=%fused_computation.52 | loop fusion | flops 2785276 | bytes 5865488 | tf_op jit(solution)/shard_map/reduce_sum | solution.py:94
  114.7 53.3 %all-reduce.6 = (f32[]{:T(128)}, f32[]{:T(128)}, f32[]{:T(128)}, f32[]{:T(128)}) all-reduce(f32[]{:T(128)} %get-tuple-element.6, f32[]{:T(128)} %get-tuple-element.8, f32[]{:T(128)} %get-tuple-element.7, f32[]{:T(128)} %get-tuple-element.5), channel_id=1, replica_groups=mesh['panel'=2,'gx'=16] {'panel','gx'}, use_global_device_ids=true, to_apply=%region_9.10 | all-reduce | flops 4 | bytes 32 | tf_op jit(solution)/shard_map/psum | solution.py:91
  172.6 0.1 multiply_add_fusion
  172.7 1.0 copy.412
  (80 shorter events, 2.2 us)
Async XLA Ops:
  0.0 2.2 %copy-start = (f32[20,64,128]{2,1,0:T(8,128)S(1)}, f32[20,64,128]{2,1,0:T(8,128)}, u32[]{:S(2)}) copy-start(f32[20,64,128]{2,1,0:T(8,128)} %param.10) | copy-start | bytes 1966084
  1.4 1.3 copy-start.3
  1.7 14.0 %collective-permute-start.2 = (f32[20,64]{1,0:T(8,128)S(1)}, f32[20,64]{1,0:T(8,128)S(1)}, u32[]{:S(2)}, u32[]{:S(2)}) collective-permute-start(f32[20,64]{1,0:T(8,128)S(1)} %bitcast.126), channel_id=1, source_target_pairs={{16,0},{0,16},{17,1},{1,17},{18,2},{2,18},{19,3},{3,19},{20,4},{4,... | collective-permute-start | bytes 15368 | tf_op jit(solution)/shard_map/ppermute | solution.py:17
  2.6 14.4 %collective-permute-start = (f32[20,128]{1,0:T(8,128)S(1)}, f32[20,128]{1,0:T(8,128)S(1)}, u32[]{:S(2)}, u32[]{:S(2)}) collective-permute-start(f32[20,128]{1,0:T(8,128)S(1)} %slice_bitcast_fusion.13), channel_id=1, source_target_pairs={{15,0},{0,1},{1,2},{2,3},{3,4},{4,5},{5,6},{6,7},{7,8},{8,9},{9,10... | collective-permute-start | bytes 30728 | tf_op jit(solution)/shard_map/ppermute | solution.py:17
  2.7 1.3 copy-start.12
  4.1 1.0 copy-start.16
  5.7 11.4 %copy-start.13 = (f32[64,128]{1,0:T(8,128)S(1)}, f32[64,128]{1,0:T(8,128)}, u32[]{:S(2)}) copy-start(f32[64,128]{1,0:T(8,128)} %param.13) | copy-start | bytes 98308
  5.7 11.4 %copy-start.14 = (f32[64,128]{1,0:T(8,128)S(1)}, f32[64,128]{1,0:T(8,128)}, u32[]{:S(2)}) copy-start(f32[64,128]{1,0:T(8,128)} %param.14) | copy-start | bytes 98308
  5.7 11.4 %copy-start.15 = (f32[20]{0:T(128)S(1)}, f32[20]{0:T(128)}, u32[]{:S(2)}) copy-start(f32[20]{0:T(128)} %param.15) | copy-start | bytes 244
  19.4 5.1 %collective-permute-start.3 = (f32[20,64]{1,0:T(8,128)S(1)}, f32[20,64]{1,0:T(8,128)S(1)}, u32[]{:S(2)}, u32[]{:S(2)}) collective-permute-start(f32[20,64]{1,0:T(8,128)S(1)} %bitcast.122), channel_id=1, source_target_pairs={{16,0},{0,16},{17,1},{1,17},{18,2},{2,18},{19,3},{3,19},{20,4},{4,... | collective-permute-start | bytes 15368 | tf_op jit(solution)/shard_map/ppermute | solution.py:17
  23.1 2.8 %collective-permute-start.1 = (f32[20,128]{1,0:T(8,128)S(1)}, f32[20,128]{1,0:T(8,128)S(1)}, u32[]{:S(2)}, u32[]{:S(2)}) collective-permute-start(f32[20,128]{1,0:T(8,128)S(1)} %slice_bitcast_fusion.12), channel_id=1, source_target_pairs={{1,0},{2,1},{3,2},{4,3},{5,4},{6,5},{7,6},{8,7},{9,8},{10,9},{11,1... | collective-permute-start | bytes 30728 | tf_op jit(solution)/shard_map/ppermute | solution.py:17
  30.1 1.0 copy-start.6
  30.1 1.1 copy-start.8
  30.1 1.2 copy-start.10
  31.3 2.1 %copy-start.4 = (f32[19,64,128]{2,1,0:T(8,128)S(1)}, f32[19,64,128]{2,1,0:T(8,128)}, u32[]{:S(2)}) copy-start(f32[19,64,128]{2,1,0:T(8,128)} %param.12) | copy-start | bytes 1867780
  35.4 3.7 %collective-permute-start.6 = (f32[20,64]{1,0:T(8,128)S(1)}, f32[20,64]{1,0:T(8,128)S(1)}, u32[]{:S(2)}, u32[]{:S(2)}) collective-permute-start(f32[20,64]{1,0:T(8,128)S(1)} %bitcast.124), channel_id=1, source_target_pairs={{16,0},{0,16},{17,1},{1,17},{18,2},{2,18},{19,3},{3,19},{20,4},{4,... | collective-permute-start | bytes 15368 | tf_op jit(solution)/shard_map/ppermute | solution.py:17
  36.9 3.6 %collective-permute-start.4 = (f32[20,128]{1,0:T(8,128)S(1)}, f32[20,128]{1,0:T(8,128)S(1)}, u32[]{:S(2)}, u32[]{:S(2)}) collective-permute-start(f32[20,128]{1,0:T(8,128)S(1)} %slice_bitcast_fusion.11), channel_id=1, source_target_pairs={{15,0},{0,1},{1,2},{2,3},{3,4},{4,5},{5,6},{6,7},{7,8},{8,9},{9,10... | collective-permute-start | bytes 30728 | tf_op jit(solution)/shard_map/ppermute | solution.py:17
  42.3 5.1 %copy-start.1 = (f32[20,64,128]{2,0,1:T(8,128)}, f32[20,64,128]{2,0,1:T(8,128)S(1)}, u32[]{:S(2)}) copy-start(f32[20,64,128]{2,0,1:T(8,128)S(1)} %get-tuple-element.26) | copy-start | bytes 1966084
  43.2 4.2 %collective-permute-start.7 = (f32[20,64]{1,0:T(8,128)}, f32[20,64]{1,0:T(8,128)}, u32[]{:S(2)}, u32[]{:S(2)}) collective-permute-start(f32[20,64]{1,0:T(8,128)} %bitcast.31), channel_id=1, source_target_pairs={{16,0},{0,16},{17,1},{1,17},{18,2},{2,18},{19,3},{3,19},{20,4},{4,... | collective-permute-start | bytes 15368 | tf_op jit(solution)/shard_map/ppermute | solution.py:17
  47.4 2.7 %collective-permute-start.5 = (f32[20,128]{1,0:T(8,128)}, f32[20,128]{1,0:T(8,128)S(1)}, u32[]{:S(2)}, u32[]{:S(2)}) collective-permute-start(f32[20,128]{1,0:T(8,128)} %slice_bitcast_fusion.10), channel_id=1, source_target_pairs={{1,0},{2,1},{3,2},{4,3},{5,4},{6,5},{7,6},{8,7},{9,8},{10,9},{11,1... | collective-permute-start | bytes 30728 | tf_op jit(solution)/shard_map/ppermute | solution.py:17
  87.3 0.9 copy-start.2
  88.3 1.0 copy-start.7
  88.3 1.1 copy-start.9
  88.3 1.2 copy-start.11
  89.4 2.1 %copy-start.5 = (f32[19,64,128]{2,1,0:T(8,128)S(1)}, f32[19,64,128]{2,1,0:T(8,128)}, u32[]{:S(2)}) copy-start(f32[19,64,128]{2,1,0:T(8,128)} %param.12) | copy-start | bytes 1867780
  93.6 3.7 %collective-permute-start.10 = (f32[20,64]{1,0:T(8,128)S(1)}, f32[20,64]{1,0:T(8,128)S(1)}, u32[]{:S(2)}, u32[]{:S(2)}) collective-permute-start(f32[20,64]{1,0:T(8,128)S(1)} %bitcast.125), channel_id=1, source_target_pairs={{16,0},{0,16},{17,1},{1,17},{18,2},{2,18},{19,3},{3,19},{20,4},{4,... | collective-permute-start | bytes 15368 | tf_op jit(solution)/shard_map/ppermute | solution.py:17
  95.8 3.1 %collective-permute-start.8 = (f32[20,128]{1,0:T(8,128)S(1)}, f32[20,128]{1,0:T(8,128)S(1)}, u32[]{:S(2)}, u32[]{:S(2)}) collective-permute-start(f32[20,128]{1,0:T(8,128)S(1)} %slice_bitcast_fusion.9), channel_id=1, source_target_pairs={{15,0},{0,1},{1,2},{2,3},{3,4},{4,5},{5,6},{6,7},{7,8},{8,9},{9,10... | collective-permute-start | bytes 30728 | tf_op jit(solution)/shard_map/ppermute | solution.py:17
  101.9 7.1 %collective-permute-start.11 = (f32[20,64]{1,0:T(8,128)S(1)}, f32[20,64]{1,0:T(8,128)S(1)}, u32[]{:S(2)}, u32[]{:S(2)}) collective-permute-start(f32[20,64]{1,0:T(8,128)S(1)} %bitcast.123), channel_id=1, source_target_pairs={{16,0},{0,16},{17,1},{1,17},{18,2},{2,18},{19,3},{3,19},{20,4},{4,... | collective-permute-start | bytes 15368 | tf_op jit(solution)/shard_map/ppermute | solution.py:17
  106.8 3.6 %collective-permute-start.9 = (f32[20,128]{1,0:T(8,128)S(1)}, f32[20,128]{1,0:T(8,128)S(1)}, u32[]{:S(2)}, u32[]{:S(2)}) collective-permute-start(f32[20,128]{1,0:T(8,128)S(1)} %slice_bitcast_fusion.8), channel_id=1, source_target_pairs={{1,0},{2,1},{3,2},{4,3},{5,4},{6,5},{7,6},{8,7},{9,8},{10,9},{11,1... | collective-permute-start | bytes 30728 | tf_op jit(solution)/shard_map/ppermute | solution.py:17
